TPU v7x, 32 devices: a whole 2x2x4 slice. The times are simulated.
32 devices in a mesh: groups: 2 (over y), seq: 4 (over z), dp: 2 (over x), fsdp: 2 (over core).
Axes of the slice: x: 2, y: 2, z: 4, core: 2. Of those that a mesh axis runs over, the one named last changes fastest.
Arguments:
- tokens: bfloat16 [8, 4, 8, 16, 1024], P(('groups', 'dp', 'fsdp'), 'seq'), parts along dimension 0, may hold values from -6 to 6
- timesteps: int32 [8], P(('groups', 'dp', 'fsdp')), parts along dimension 0, may hold values from 0 to 999
- pxrd_mod: float32 [8, 3, 1024], P(('groups', 'dp', 'fsdp')), parts along dimension 0, may hold values from -3 to 3
- time_weight: bfloat16 [256, 3072], P('fsdp'), may hold values from -0.375 to 0.375
- conv_kernel: float32 [27, 1024], replicated, may hold values from -0.9 to 0.9
- qkv_weight: bfloat16 [1024, 1536], P('fsdp'), may hold values from -0.75 to 0.75
- out_weight: bfloat16 [512, 1024], P('fsdp'), may hold values from -1 to 1
- out_cot: bfloat16 [8, 4, 8, 16, 1024], P(('groups', 'dp', 'fsdp'), 'seq'), parts along dimension 0, may hold values from -6 to 6
Outputs:
- out_tokens: bfloat16 [8, 4, 8, 16, 1024], P(('groups', 'dp', 'fsdp'), 'seq'), parts along dimension 0
- d_tokens: bfloat16 [8, 4, 8, 16, 1024], P(('groups', 'dp', 'fsdp'), 'seq'), parts along dimension 0
- d_kernel: float32 [54, 1024], P('groups'), parts along dimension 0
There are 2 independent parts, one for each index of `groups`. A program takes and returns all parts, laid end to end along the dimension named above; an argument that names none is the same for every part. Nothing has to cross between parts.
All inputs are finite; a program needn't handle non-finite values.
Results may differ from a plain program's by a relative error of at most 0.024.
Values may be sent and summed in bfloat16 or wider, within the bound.
No kernel may reach another device: no remote copies, remote signals or barrier semaphores. Data moves between devices by JAX's collectives and lax.ppermute only.
A program may use at most 64 MiB of HBM per device.

v0:
```python
import math
import jax
import jax.numpy as jnp
from jax import lax
from jax.sharding import PartitionSpec as P

H = 8
HD = 64


def padded_2(value, sides, width):
    for axis, dim in sides:
        count, length = (lax.axis_size(axis), value.shape[dim])
        up = [(i, (i + 1) % count) for i in range(count - 1)]
        down = [(j, i) for i, j in up]
        last = lax.slice_in_dim(value, length - width, length, axis=dim)
        leading = lax.slice_in_dim(value, 0, width, axis=dim)
        before = lax.ppermute(last, axis, up)
        after = lax.ppermute(leading, axis, down)
        value = jnp.concatenate([before, value, after], axis=dim)
    return value


def time_features(steps_int, freq_width):
    half_width = freq_width // 2
    freq_index = jnp.arange(half_width).astype(jnp.float32)
    frequency = jnp.exp(freq_index * (-math.log(10000.0) / half_width))
    angles = steps_int.astype(jnp.float32)[:, None] * frequency[None, :]
    return jnp.concatenate([jnp.cos(angles), jnp.sin(angles)], axis=1).astype(jnp.bfloat16)


def modulation(steps_int, pxrd_mod, time_weight):
    features = time_features(steps_int, time_weight.shape[0])
    projected = jnp.dot(features, time_weight, preferred_element_type=jnp.float32)
    return projected.reshape(steps_int.shape[0], 3, time_weight.shape[1] // 3) + pxrd_mod


def depthwise(padded_z, kernel_taps, plane_count):
    framed = jnp.pad(padded_z, ((0, 0), (1, 1), (1, 1), (0, 0)))
    side_y = framed.shape[1] - 2
    side_x = framed.shape[2] - 2
    result = jnp.zeros((plane_count, side_y, side_x, framed.shape[3]), jnp.float32)
    for tap_z in range(3):
        for tap_y in range(3):
            for tap_x in range(3):
                window = framed[
                    tap_z : tap_z + plane_count, tap_y : tap_y + side_y, tap_x : tap_x + side_x
                ]
                result = result + kernel_taps[9 * tap_z + 3 * tap_y + tap_x] * window.astype(
                    jnp.float32
                )
    return result


def kernel_terms(padded_z, upstream, plane_count):
    framed = jnp.pad(padded_z, ((0, 0), (1, 1), (1, 1), (0, 0)))
    side_y = framed.shape[1] - 2
    side_x = framed.shape[2] - 2
    upstream_f = upstream.astype(jnp.float32)
    collected = []
    for tap_z in range(3):
        for tap_y in range(3):
            for tap_x in range(3):
                window = framed[
                    tap_z : tap_z + plane_count, tap_y : tap_y + side_y, tap_x : tap_x + side_x
                ]
                collected.append(jnp.sum(window.astype(jnp.float32) * upstream_f, axis=(0, 1, 2)))
    return jnp.stack(collected)


def modulate(stream, shift_row, scale_row):
    centre = stream - jnp.mean(stream, axis=-1, keepdims=True)
    spread = jnp.mean(centre * centre, axis=-1, keepdims=True)
    return centre * lax.rsqrt(spread + 1e-06) * (1.0 + scale_row) + shift_row


def head_norms(projected):
    row_count = projected.shape[0]
    sections = projected.reshape(row_count, 3, H, HD)
    query_key = sections[:, :2]
    normed = query_key * lax.rsqrt(jnp.mean(query_key * query_key, axis=-1, keepdims=True) + 1e-06)
    return (
        normed[:, 0].reshape(row_count, H * HD),
        normed[:, 1].reshape(row_count, H * HD),
        sections[:, 2].reshape(row_count, H * HD),
    )


def attend_both(queries, grads, key_rows, value_rows):
    count = queries.shape[0]
    heads = queries.shape[1]
    block = min(512, count)
    steps = count // block
    scale_dot = 1.0 / math.sqrt(HD)

    def one_block(carry, pieces):
        query_blk, grad_blk = pieces
        scores = (
            jnp.einsum("qhd,khd->hqk", query_blk, key_rows, preferred_element_type=jnp.float32)
            * scale_dot
        )
        expo = jnp.exp(scores)
        totals = jnp.sum(expo, axis=-1, keepdims=True)
        weights = expo / totals
        probs = weights.astype(jnp.bfloat16)
        attn_blk = jnp.einsum(
            "hqk,khd->qhd", probs, value_rows, preferred_element_type=jnp.float32
        ).astype(jnp.bfloat16)
        delta = jnp.sum(grad_blk.astype(jnp.float32) * attn_blk.astype(jnp.float32), axis=-1).T
        dprob = jnp.einsum("qhd,khd->hqk", grad_blk, value_rows, preferred_element_type=jnp.float32)
        dscore = (weights * (dprob - delta[:, :, None]) * scale_dot).astype(jnp.bfloat16)
        dquery = jnp.einsum("hqk,khd->qhd", dscore, key_rows, preferred_element_type=jnp.float32)
        dkey = carry[0] + jnp.einsum(
            "hqk,qhd->khd", dscore, query_blk, preferred_element_type=jnp.float32
        )
        dvalue = carry[1] + jnp.einsum(
            "hqk,qhd->khd", probs, grad_blk, preferred_element_type=jnp.float32
        )
        return ((dkey, dvalue), (attn_blk, dquery))

    zeros_kv = jnp.zeros(key_rows.shape, jnp.float32)
    (dkey, dvalue), (attn_all, dquery) = lax.scan(
        one_block,
        (zeros_kv, zeros_kv),
        (queries.reshape(steps, block, heads, HD), grads.reshape(steps, block, heads, HD)),
    )
    return (attn_all.reshape(count, heads, HD), dquery.reshape(count, heads, HD), dkey, dvalue)


def shards(tokens, timesteps, pxrd_mod, time_weight, conv_kernel, qkv_weight, out_weight, out_cot):
    w_qkv, w_out, w_time = (
        lax.all_gather(qkv_weight, "fsdp", axis=0, tiled=True),
        lax.all_gather(out_weight, "fsdp", axis=0, tiled=True),
        lax.all_gather(time_weight, "fsdp", axis=0, tiled=True),
    )
    plane_count = tokens.shape[1]
    side_y = tokens.shape[2]
    side_x = tokens.shape[3]
    width_model = tokens.shape[4]
    row_count = plane_count * side_y * side_x
    inner_width = H * HD
    seq_count = lax.axis_size("seq")
    head_groups = min(H, seq_count)
    per_device = H // head_groups
    row_split = seq_count // head_groups
    part_rows = row_count // row_split
    group_width = per_device * HD
    padded = padded_2(tokens, (("seq", 1),), 1)[0]
    mixed = depthwise(padded, conv_kernel, plane_count)
    resid = (
        (tokens[0].astype(jnp.float32) + mixed).astype(jnp.bfloat16).reshape(row_count, width_model)
    )
    modul = modulation(timesteps, pxrd_mod, w_time)
    shift_row = modul[0, 0]
    scale_row = modul[0, 1]
    gate_row = modul[0, 2]
    resid_f = resid.astype(jnp.float32)
    normed = modulate(resid_f, shift_row, scale_row).astype(jnp.bfloat16)
    projected = jnp.dot(normed, w_qkv, preferred_element_type=jnp.float32)
    query_f, key_f, value_f = head_norms(projected)
    cotangent = out_cot[0].reshape(row_count, width_model).astype(jnp.float32)
    gated = (gate_row * cotangent).astype(jnp.bfloat16)
    grad_attn = lax.dot_general(
        gated, w_out, (((1,), (1,)), ((), ())), preferred_element_type=jnp.float32
    ).astype(jnp.bfloat16)

    def to_heads(token_rows):
        shaped = token_rows.reshape(row_split, part_rows, head_groups, group_width)
        return shaped.transpose(2, 0, 1, 3).reshape(seq_count, part_rows, group_width)

    def from_heads(head_rows):
        shaped = head_rows.reshape(head_groups, row_split, part_rows, group_width)
        return shaped.transpose(1, 2, 0, 3).reshape(row_count, inner_width)

    query_heads, grad_heads = (
        lax.all_to_all(
            to_heads(query_f.astype(jnp.bfloat16)), "seq", split_axis=0, concat_axis=0, tiled=True
        ),
        lax.all_to_all(to_heads(grad_attn), "seq", split_axis=0, concat_axis=0, tiled=True),
    )
    query_count = seq_count * part_rows
    query_heads = query_heads.reshape(query_count, per_device, HD)
    grad_heads = grad_heads.reshape(query_count, per_device, HD)
    stacked = jnp.stack(
        [
            key_f.astype(jnp.bfloat16).reshape(row_count, head_groups, group_width),
            value_f.astype(jnp.bfloat16).reshape(row_count, head_groups, group_width),
        ],
        axis=2,
    )
    by_group = stacked.transpose(1, 0, 2, 3).reshape(head_groups, row_count, 2 * group_width)
    copies = jnp.broadcast_to(
        by_group[:, None], (head_groups, row_split, row_count, 2 * group_width)
    )
    arrived = lax.all_to_all(
        copies.reshape(seq_count, row_count, 2 * group_width),
        "seq",
        split_axis=0,
        concat_axis=0,
        tiled=True,
    )
    key_value = arrived.reshape(seq_count * row_count, 2, per_device, HD)
    attn_heads, dquery, dkey, dvalue = attend_both(
        query_heads, grad_heads, key_value[:, 0], key_value[:, 1]
    )
    attn_tok = from_heads(
        lax.all_to_all(
            attn_heads.reshape(seq_count, part_rows, group_width),
            "seq",
            split_axis=0,
            concat_axis=0,
            tiled=True,
        )
    )
    projected_out = jnp.dot(attn_tok, w_out, preferred_element_type=jnp.float32)
    out_rows = (resid_f + gate_row * projected_out).astype(jnp.bfloat16)
    dquery_tok = from_heads(
        lax.all_to_all(
            dquery.reshape(seq_count, part_rows, group_width),
            "seq",
            split_axis=0,
            concat_axis=0,
            tiled=True,
        )
    )
    grads_kv = jnp.stack([dkey, dvalue], axis=1)
    returned = lax.all_to_all(
        grads_kv.reshape(seq_count, row_count, 2 * group_width).astype(jnp.bfloat16),
        "seq",
        split_axis=0,
        concat_axis=0,
        tiled=True,
    ).astype(jnp.float32)
    summed = jnp.sum(returned.reshape(head_groups, row_split, row_count, 2 * group_width), axis=1)
    grads_tok = (
        summed.reshape(head_groups, row_count, 2, group_width)
        .transpose(2, 1, 0, 3)
        .reshape(2, row_count, inner_width)
    )
    _, pullback = jax.vjp(head_norms, projected)
    (grad_projected,) = pullback((dquery_tok, grads_tok[0], grads_tok[1]))
    grad_proj_b = grad_projected.astype(jnp.bfloat16)
    grad_normed = lax.dot_general(
        grad_proj_b, w_qkv, (((1,), (1,)), ((), ())), preferred_element_type=jnp.float32
    )
    _, pull_norm = jax.vjp(lambda stream: modulate(stream, shift_row, scale_row), resid_f)
    (grad_stream,) = pull_norm(grad_normed)
    grad_resid = (
        (cotangent + grad_stream)
        .astype(jnp.bfloat16)
        .reshape(1, plane_count, side_y, side_x, width_model)
    )
    grad_padded = padded_2(grad_resid, (("seq", 1),), 1)[0]
    grad_tokens = (
        grad_resid[0].astype(jnp.float32) + depthwise(grad_padded, conv_kernel[::-1], plane_count)
    ).astype(jnp.bfloat16)
    local_terms = kernel_terms(padded, grad_resid[0], plane_count)
    norm_factor = 1.0 / math.sqrt(
        lax.axis_size("dp") * lax.axis_size("fsdp") * seq_count * row_count
    )
    grad_kernel = lax.psum(local_terms, ("seq", "dp", "fsdp")) * norm_factor
    return (out_rows.reshape(tokens.shape), grad_tokens.reshape(tokens.shape), grad_kernel)


def solution(mesh):
    placed = (
        P(("groups", "dp", "fsdp"), "seq", None, None, None),
        P(("groups", "dp", "fsdp")),
        P(("groups", "dp", "fsdp"), None, None),
        P("fsdp", None),
        P(),
        P("fsdp", None),
        P("fsdp", None),
        P(("groups", "dp", "fsdp"), "seq", None, None, None),
    )
    return jax.shard_map(
        shards,
        mesh=mesh,
        in_specs=placed,
        out_specs=(
            P(("groups", "dp", "fsdp"), "seq", None, None, None),
            P(("groups", "dp", "fsdp"), "seq", None, None, None),
            P("groups", None),
        ),
        check_vma=False,
    )
```

profile of v0, /device:TPU:8, one launch (start us, length us, event | category | flops | bytes accessed | tf_op | source)
XLA Modules:
  0.0 221.3 jit_solution(6687539041669319922)
XLA Ops:
  7.2 2.3 %copy.35 = bf16[128,3072]{0,1:T(8,128)(2,1)} copy(bf16[128,3072]{1,0:T(8,128)(2,1)} %param.11) | data formatting | bytes 1572864 | tf_op args[3]
  9.6 0.7 all-gather.8.cloned.1.call-update
  10.3 0.7 all-gather.6.cloned.1.call-update
  11.0 3.5 %collective-permute-start = (bf16[1,1,8,16,1024]{4,3,2,1,0:T(8,128)(2,1)S(1)}, bf16[1,1,8,16,1024]{4,3,2,1,0:T(8,128)(2,1)S(1)}, u32[]{:S(2)}, u32[]{:S(2)}) collective-permute-start(bf16[1,1,8,16,1024]{4,3,2,1,0:T(8,128)(2,1)S(1)} %copy-done.6), channel_id=1, source_target_pairs={{0,4},{4,8},{8,12},{1,5},{5,9},{9,13},{2,6},{6,10},{10,14},{3,7},{... | collective-permute-start | bytes 786440 | tf_op jit(solution)/shard_map/ppermute | solution.py:18
  14.5 2.4 %collective-permute-start.1 = (bf16[1,1,8,16,1024]{4,3,2,1,0:T(8,128)(2,1)S(1)}, bf16[1,1,8,16,1024]{4,3,2,1,0:T(8,128)(2,1)S(1)}, u32[]{:S(2)}, u32[]{:S(2)}) collective-permute-start(bf16[1,1,8,16,1024]{4,3,2,1,0:T(8,128)(2,1)S(1)} %copy-done.6), channel_id=1, source_target_pairs={{4,0},{8,4},{12,8},{5,1},{9,5},{13,9},{6,2},{10,6},{14,10},{7,3},{... | collective-permute-start | bytes 786440 | tf_op jit(solution)/shard_map/ppermute | solution.py:19
  18.0 3.0 %collective-permute-done = bf16[1,1,8,16,1024]{4,3,2,1,0:T(8,128)(2,1)S(1)} collective-permute-done((bf16[1,1,8,16,1024]{4,3,2,1,0:T(8,128)(2,1)S(1)}, bf16[1,1,8,16,1024]{4,3,2,1,0:T(8,128)(2,1)S(1)}, u32[]{:S(2)}, u32[]{:S(2)}) %collective-permute-start) | collective-permute-done | bytes 262176 | tf_op jit(solution)/shard_map/ppermute | solution.py:18
  21.0 3.2 %collective-permute-done.1 = bf16[1,1,8,16,1024]{4,3,2,1,0:T(8,128)(2,1)S(1)} collective-permute-done((bf16[1,1,8,16,1024]{4,3,2,1,0:T(8,128)(2,1)S(1)}, bf16[1,1,8,16,1024]{4,3,2,1,0:T(8,128)(2,1)S(1)}, u32[]{:S(2)}, u32[]{:S(2)}) %collective-permute-start.1) | collective-permute-done | bytes 262176 | tf_op jit(solution)/shard_map/ppermute | solution.py:19
  24.2 0.1 maximum_bitcast_fusion
  24.3 0.9 copy-done.1
  25.2 2.7 %convert_reduce_fusion = (f32[8,16]{1,0:T(8,128)S(1)}, bf16[1,8,16,1024]{3,2,1,0:T(8,128)(2,1)S(1)}) fusion(f32[1024]{0:T(1024)S(1)} %bitcast.275, f32[1024]{0:T(1024)S(1)} %bitcast.277, f32[1024]{0:T(1024)S(1)} %bitcast.281, f32[1024]{0:T(1024)S(1)} %bitcast.283, bf16[1,1,8,16,1024]{4,3,2,1,0:T(8,128)(2,1)S(1)} %collective-permute-done.1, ...), kind=kLoop, calls=%fused_computation.221 | loop fusion | flops 11009920 | bytes 1946112 | tf_op jit(solution)/shard_map/reduce_sum | solution.py:72
  28.2 0.2 multiply_reduce_fusion.3
  28.4 0.6 multiply_add_fusion.1
  29.0 2.0 fusion.103
  31.1 1.5 all-gather.8.cloned.1.call-done
  32.6 1.7 convolution_convert_fusion.2
  34.3 0.8 copy.58
  35.1 5.2 %all-to-all-start.3 = ((bf16[4,128,128]{1,2,0:T(8,128)(2,1)}), bf16[4,128,128]{1,2,0:T(8,128)(2,1)S(1)}, u32[]{:S(2)}, u32[]{:S(2)}) async-start(bf16[4,128,128]{1,2,0:T(8,128)(2,1)} %bitcast.65), calls=%async_computation.3 | async-start | bytes 262144 | tf_op jit(solution)/shard_map/all_to_all | solution.py:179
  40.2 0.9 add_convert_fusion.1
  41.2 6.3 %all-gather.6.cloned.1.call-done = bf16[1024,1536]{1,0:T(8,128)(2,1)} async-done(((bf16[512,1536]{1,0:T(8,128)(2,1)}), bf16[1024,1536]{1,0:T(8,128)(2,1)}) %all-gather.6.cloned.1.call-update) | async-done | bytes 3145744 | tf_op jit(solution)/shard_map/all_gather | solution.py:132
  47.5 3.2 %copy.36 = bf16[1536,1024]{1,0:T(8,128)(2,1)S(1)} copy(bf16[1536,1024]{0,1:T(8,128)(2,1)} %bitcast.242) | data formatting | bytes 6291456 | tf_op jit(solution)/shard_map/dot_general | solution.py:159
  50.7 1.9 fusion.104
  52.7 0.8 copy-done.3
  53.6 0.7 fusion.98
  54.2 5.1 %all-to-all-start.1 = ((bf16[4,128,128]{1,2,0:T(8,128)(2,1)}), bf16[4,128,128]{1,2,0:T(8,128)(2,1)S(1)}, u32[]{:S(2)}, u32[]{:S(2)}) async-start(bf16[4,128,128]{1,2,0:T(8,128)(2,1)} %bitcast.54), calls=%async_computation.1 | async-start | bytes 262144 | tf_op jit(solution)/shard_map/all_to_all | solution.py:176
  59.4 1.0 slice.712
  60.3 0.7 pad_maximum_fusion
  61.1 3.6 %all-to-all-done.1 = bf16[4,128,128]{1,2,0:T(8,128)(2,1)S(1)} async-done(((bf16[4,128,128]{1,2,0:T(8,128)(2,1)}), bf16[4,128,128]{1,2,0:T(8,128)(2,1)S(1)}, u32[]{:S(2)}, u32[]{:S(2)}) %all-to-all-start.1) | async-done | bytes 131104 | tf_op jit(solution)/shard_map/all_to_all | solution.py:176
  64.6 4.5 %all-to-all-start = ((bf16[4,128,256]{1,2,0:T(8,128)(2,1)}), bf16[4,128,256]{1,2,0:T(8,128)(2,1)S(1)}, u32[]{:S(2)}, u32[]{:S(2)}) async-start(bf16[4,128,256]{1,2,0:T(8,128)(2,1)} %bitcast.50), calls=%async_computation | async-start | bytes 524288 | tf_op jit(solution)/shard_map/all_to_all | solution.py:195
  69.1 0.1 copy.44
  69.3 0.1 copy.40
  69.5 6.0 %all-to-all-done = bf16[4,128,256]{1,2,0:T(8,128)(2,1)S(1)} async-done(((bf16[4,128,256]{1,2,0:T(8,128)(2,1)}), bf16[4,128,256]{1,2,0:T(8,128)(2,1)S(1)}, u32[]{:S(2)}, u32[]{:S(2)}) %all-to-all-start) | async-done | bytes 262176 | tf_op jit(solution)/shard_map/all_to_all | solution.py:195
  75.4 0.2 copy.39
  75.7 0.1 reshape.516
  75.8 0.5 fusion.1
  76.3 0.3 fusion.7
  76.6 0.4 fusion.6
  77.1 0.3 multiply_reduce_fusion.4
  77.4 0.7 multiply_convert_fusion
  78.1 0.4 fusion.5
  78.6 0.7 copy.48
  79.4 5.2 %all-to-all-start.4 = ((bf16[4,128,256]{1,2,0:T(8,128)(2,1)}), bf16[4,128,256]{1,2,0:T(8,128)(2,1)S(1)}, u32[]{:S(2)}, u32[]{:S(2)}) async-start(bf16[4,128,256]{1,2,0:T(8,128)(2,1)} %copy.48), calls=%async_computation.4 | async-start | bytes 524288 | tf_op jit(solution)/shard_map/all_to_all | solution.py:227
  84.6 0.1 div.54
  84.8 0.3 convolution_bitcast_fusion
  85.1 0.1 reshape_reshape.12
  85.2 0.7 copy.50
  85.9 0.7 copy.42
  86.6 4.2 %all-to-all-done.4 = bf16[4,128,256]{1,2,0:T(8,128)(2,1)S(1)} async-done(((bf16[4,128,256]{1,2,0:T(8,128)(2,1)}), bf16[4,128,256]{1,2,0:T(8,128)(2,1)S(1)}, u32[]{:S(2)}, u32[]{:S(2)}) %all-to-all-start.4) | async-done | bytes 262176 | tf_op jit(solution)/shard_map/all_to_all | solution.py:227
  90.8 4.0 %all-to-all-start.5 = ((f32[4,128,128]{1,2,0:T(8,128)}), f32[4,128,128]{1,2,0:T(8,128)S(1)}, u32[]{:S(2)}, u32[]{:S(2)}) async-start(f32[4,128,128]{1,2,0:T(8,128)} %copy.50), calls=%async_computation.5 | async-start | bytes 524288 | tf_op jit(solution)/shard_map/all_to_all | solution.py:218
  94.9 6.1 %all-to-all-done.5 = f32[4,128,128]{1,2,0:T(8,128)S(1)} async-done(((f32[4,128,128]{1,2,0:T(8,128)}), f32[4,128,128]{1,2,0:T(8,128)S(1)}, u32[]{:S(2)}, u32[]{:S(2)}) %all-to-all-start.5) | async-done | bytes 262176 | tf_op jit(solution)/shard_map/all_to_all | solution.py:218
  101.0 4.0 %all-to-all-start.2 = ((bf16[4,128,128]{1,2,0:T(8,128)(2,1)}), bf16[4,128,128]{1,2,0:T(8,128)(2,1)S(1)}, u32[]{:S(2)}, u32[]{:S(2)}) async-start(bf16[4,128,128]{1,2,0:T(8,128)(2,1)} %copy.42), calls=%async_computation.2 | async-start | bytes 262144 | tf_op jit(solution)/shard_map/all_to_all | solution.py:207
  105.1 0.1 add_add_fusion.1
  105.3 1.6 copy-done
  107.0 1.2 multiply_reduce_fusion
  108.2 0.3 fusion.94
  108.6 1.3 fusion.75
  109.8 1.9 collective-permute-start.3
  111.8 4.1 %collective-permute-start.2 = (bf16[1,1,8,16,1024]{4,3,2,1,0:T(8,128)(2,1)S(1)}, bf16[1,1,8,16,1024]{4,3,2,1,0:T(8,128)(2,1)S(1)}, u32[]{:S(2)}, u32[]{:S(2)}) collective-permute-start(bf16[1,1,8,16,1024]{4,3,2,1,0:T(8,128)(2,1)S(1)} %bitcast.245), channel_id=1, source_target_pairs={{0,4},{4,8},{8,12},{1,5},{5,9},{9,13},{2,6},{6,10},{10,14},{3,7},{... | collective-permute-start | bytes 786440 | tf_op jit(solution)/shard_map/ppermute | solution.py:18
  115.9 1.6 fusion.76
  117.5 2.6 %stack.130 = f32[27,1024]{1,0:T(8,128)} concatenate(f32[1,1024]{1,0:T(1,128)S(1)} %bitcast.331, f32[1,1024]{1,0:T(1,128)S(1)} %bitcast.332, f32[1,1024]{1,0:T(1,128)S(1)} %bitcast.333, f32[1,1024]{1,0:T(1,128)S(1)} %bitcast.334, f32[1,1024]{1,0:T(1,128)S(1)} %bitcast.329, f32[1,1024]{1,0:T(1,128)S(1)} %bitcast.335, f32[1,1024]{1,0:T(1,128)S(1)} %bitcast.336, ...), dimensions={0} | concatenate | bytes 221184 | tf_op jit(solution)/shard_map/stack | solution.py:68
  120.4 1.0 fusion.3
  121.5 88.4 %all-reduce.8.cloned.1.call-done = f32[27,1024]{1,0:T(8,128)} async-done(((f32[27,1024]{1,0:T(8,128)}), f32[27,1024]{1,0:T(8,128)}) %all-reduce.8.cloned.1.call-update) | async-done | bytes 110608 | tf_op jit(solution)/shard_map/psum | solution.py:261
  209.9 1.6 broadcast_multiply_fusion
  211.4 0.1 maximum_bitcast_fusion.1
  211.8 3.0 %fusion.90 = bf16[1,1,8,16,1024]{4,3,2,1,0:T(8,128)(2,1)} fusion(bf16[3,8,16,1024]{3,2,1,0:T(8,128)(2,1)S(1)} %maximum_bitcast_fusion.1, f32[1024]{0:T(1024)S(1)} %bitcast.280, f32[1024]{0:T(1024)S(1)} %bitcast.264, f32[1024]{0:T(1024)S(1)} %bitcast.274, f32[1024]{0:T(1024)S(1)} %bitcast.272, bf16[1,1,8,16,1024]{4,3,2,1,0:T(8,128)(2,1)S(1)} %collective-permute-done.3, ...), kind=kLoop, calls=%fused_computation.227 | loop fusion | flops 10747904 | bytes 1945600 | tf_op jit(solution)/shard_map/reshape | solution.py:262
  (171 shorter events, 1.3 us)
Async XLA Ops:
  7.2 21.9 %all-gather.4.cloned.1.call-start = ((), (), s32[]{:S(2)}) async-start(), calls=%async_computation.6 | async-start | bytes 2359296 | tf_op jit(solution)/shard_map/all_gather | solution.py:134
  9.5 23.0 %all-gather.8.cloned.1.call-start = ((), (), s32[]{:S(2)}) async-start(), calls=%async_computation.8 | async-start | bytes 1572864 | tf_op jit(solution)/shard_map/all_gather | solution.py:133
  10.3 37.2 %all-gather.6.cloned.1.call-start = ((), (), s32[]{:S(2)}) async-start(), calls=%async_computation.7 | async-start | bytes 4718592 | tf_op jit(solution)/shard_map/all_gather | solution.py:132
  11.0 9.9 %collective-permute-start = (bf16[1,1,8,16,1024]{4,3,2,1,0:T(8,128)(2,1)S(1)}, bf16[1,1,8,16,1024]{4,3,2,1,0:T(8,128)(2,1)S(1)}, u32[]{:S(2)}, u32[]{:S(2)}) collective-permute-start(bf16[1,1,8,16,1024]{4,3,2,1,0:T(8,128)(2,1)S(1)} %copy-done.6), channel_id=1, source_target_pairs={{0,4},{4,8},{8,12},{1,5},{5,9},{9,13},{2,6},{6,10},{10,14},{3,7},{... | collective-permute-start | bytes 786440 | tf_op jit(solution)/shard_map/ppermute | solution.py:18
  14.5 9.7 %collective-permute-start.1 = (bf16[1,1,8,16,1024]{4,3,2,1,0:T(8,128)(2,1)S(1)}, bf16[1,1,8,16,1024]{4,3,2,1,0:T(8,128)(2,1)S(1)}, u32[]{:S(2)}, u32[]{:S(2)}) collective-permute-start(bf16[1,1,8,16,1024]{4,3,2,1,0:T(8,128)(2,1)S(1)} %copy-done.6), channel_id=1, source_target_pairs={{4,0},{8,4},{12,8},{5,1},{9,5},{13,9},{6,2},{10,6},{14,10},{7,3},{... | collective-permute-start | bytes 786440 | tf_op jit(solution)/shard_map/ppermute | solution.py:19
  17.7 10.3 %copy-start.15 = (f32[1,1024]{1,0:T(1,128)}, f32[1,1024]{1,0:T(1,128)S(1)}, u32[]{:S(2)}) copy-start(f32[1,1024]{1,0:T(1,128)S(1)} %get-tuple-element.86) | copy-start | bytes 12292
  17.7 10.3 %copy-start.17 = (f32[1,1024]{1,0:T(1,128)}, f32[1,1024]{1,0:T(1,128)S(1)}, u32[]{:S(2)}) copy-start(f32[1,1024]{1,0:T(1,128)S(1)} %get-tuple-element.87) | copy-start | bytes 12292
  17.7 10.3 %copy-start.19 = (f32[1,1024]{1,0:T(1,128)}, f32[1,1024]{1,0:T(1,128)S(1)}, u32[]{:S(2)}) copy-start(f32[1,1024]{1,0:T(1,128)S(1)} %get-tuple-element.88) | copy-start | bytes 12292
  17.7 10.3 %copy-start.21 = (f32[1,1024]{1,0:T(1,128)}, f32[1,1024]{1,0:T(1,128)S(1)}, u32[]{:S(2)}) copy-start(f32[1,1024]{1,0:T(1,128)S(1)} %get-tuple-element.89) | copy-start | bytes 12292
  17.7 10.3 %copy-start.23 = (f32[1,1024]{1,0:T(1,128)}, f32[1,1024]{1,0:T(1,128)S(1)}, u32[]{:S(2)}) copy-start(f32[1,1024]{1,0:T(1,128)S(1)} %get-tuple-element.90) | copy-start | bytes 12292
  17.8 10.2 %copy-start.25 = (f32[1,1024]{1,0:T(1,128)}, f32[1,1024]{1,0:T(1,128)S(1)}, u32[]{:S(2)}) copy-start(f32[1,1024]{1,0:T(1,128)S(1)} %get-tuple-element.64) | copy-start | bytes 12292
  17.8 10.2 %copy-start.27 = (f32[1,1024]{1,0:T(1,128)}, f32[1,1024]{1,0:T(1,128)S(1)}, u32[]{:S(2)}) copy-start(f32[1,1024]{1,0:T(1,128)S(1)} %get-tuple-element.65) | copy-start | bytes 12292
  17.8 10.2 %copy-start.29 = (f32[1,1024]{1,0:T(1,128)}, f32[1,1024]{1,0:T(1,128)S(1)}, u32[]{:S(2)}) copy-start(f32[1,1024]{1,0:T(1,128)S(1)} %get-tuple-element.66) | copy-start | bytes 12292
  17.8 10.2 %copy-start.31 = (f32[1,1024]{1,0:T(1,128)}, f32[1,1024]{1,0:T(1,128)S(1)}, u32[]{:S(2)}) copy-start(f32[1,1024]{1,0:T(1,128)S(1)} %get-tuple-element.67) | copy-start | bytes 12292
  17.8 10.2 %copy-start.33 = (f32[1,1024]{1,0:T(1,128)}, f32[1,1024]{1,0:T(1,128)S(1)}, u32[]{:S(2)}) copy-start(f32[1,1024]{1,0:T(1,128)S(1)} %get-tuple-element.68) | copy-start | bytes 12292
  17.9 10.2 %copy-start.35 = (f32[1,1024]{1,0:T(1,128)}, f32[1,1024]{1,0:T(1,128)S(1)}, u32[]{:S(2)}) copy-start(f32[1,1024]{1,0:T(1,128)S(1)} %get-tuple-element.69) | copy-start | bytes 12292
  17.9 10.2 %copy-start.37 = (f32[1,1024]{1,0:T(1,128)}, f32[1,1024]{1,0:T(1,128)S(1)}, u32[]{:S(2)}) copy-start(f32[1,1024]{1,0:T(1,128)S(1)} %get-tuple-element.70) | copy-start | bytes 12292
  17.9 10.2 %copy-start.39 = (f32[1,1024]{1,0:T(1,128)}, f32[1,1024]{1,0:T(1,128)S(1)}, u32[]{:S(2)}) copy-start(f32[1,1024]{1,0:T(1,128)S(1)} %get-tuple-element.71) | copy-start | bytes 12292
  17.9 10.2 %copy-start.41 = (f32[1,1024]{1,0:T(1,128)}, f32[1,1024]{1,0:T(1,128)S(1)}, u32[]{:S(2)}) copy-start(f32[1,1024]{1,0:T(1,128)S(1)} %get-tuple-element.72) | copy-start | bytes 12292
  17.9 10.2 %copy-start.43 = (f32[1,1024]{1,0:T(1,128)}, f32[1,1024]{1,0:T(1,128)S(1)}, u32[]{:S(2)}) copy-start(f32[1,1024]{1,0:T(1,128)S(1)} %get-tuple-element.73) | copy-start | bytes 12292
  17.9 10.2 %copy-start.45 = (f32[1,1024]{1,0:T(1,128)}, f32[1,1024]{1,0:T(1,128)S(1)}, u32[]{:S(2)}) copy-start(f32[1,1024]{1,0:T(1,128)S(1)} %get-tuple-element.74) | copy-start | bytes 12292
  17.9 10.2 %copy-start.47 = (f32[1,1024]{1,0:T(1,128)}, f32[1,1024]{1,0:T(1,128)S(1)}, u32[]{:S(2)}) copy-start(f32[1,1024]{1,0:T(1,128)S(1)} %get-tuple-element.75) | copy-start | bytes 12292
  17.9 10.2 %copy-start.49 = (f32[1,1024]{1,0:T(1,128)}, f32[1,1024]{1,0:T(1,128)S(1)}, u32[]{:S(2)}) copy-start(f32[1,1024]{1,0:T(1,128)S(1)} %get-tuple-element.76) | copy-start | bytes 12292
  17.9 10.2 %copy-start.51 = (f32[1,1024]{1,0:T(1,128)}, f32[1,1024]{1,0:T(1,128)S(1)}, u32[]{:S(2)}) copy-start(f32[1,1024]{1,0:T(1,128)S(1)} %get-tuple-element.77) | copy-start | bytes 12292
  17.9 10.2 %copy-start.53 = (f32[1,1024]{1,0:T(1,128)}, f32[1,1024]{1,0:T(1,128)S(1)}, u32[]{:S(2)}) copy-start(f32[1,1024]{1,0:T(1,128)S(1)} %get-tuple-element.78) | copy-start | bytes 12292
  18.0 10.2 %copy-start.55 = (f32[1,1024]{1,0:T(1,128)}, f32[1,1024]{1,0:T(1,128)S(1)}, u32[]{:S(2)}) copy-start(f32[1,1024]{1,0:T(1,128)S(1)} %get-tuple-element.79) | copy-start | bytes 12292
  31.1 16.4 %copy-start.63 = (f32[1,1,1024]{2,0,1:T(1,128)}, f32[1,1,1024]{2,0,1:T(1,128)S(1)}, u32[]{:S(2)}) copy-start(f32[1,1,1024]{2,0,1:T(1,128)S(1)} %get-tuple-element.91) | copy-start | bytes 12292
  31.1 16.4 %copy-start.65 = (f32[1,1,1024]{2,0,1:T(1,128)}, f32[1,1,1024]{2,0,1:T(1,128)S(1)}, u32[]{:S(2)}) copy-start(f32[1,1,1024]{2,0,1:T(1,128)S(1)} %get-tuple-element.93) | copy-start | bytes 12292
  35.1 19.2 %all-to-all-start.3 = ((bf16[4,128,128]{1,2,0:T(8,128)(2,1)}), bf16[4,128,128]{1,2,0:T(8,128)(2,1)S(1)}, u32[]{:S(2)}, u32[]{:S(2)}) async-start(bf16[4,128,128]{1,2,0:T(8,128)(2,1)} %bitcast.65), calls=%async_computation.3 | async-start | bytes 262144 | tf_op jit(solution)/shard_map/all_to_all | solution.py:179
  54.2 10.4 %all-to-all-start.1 = ((bf16[4,128,128]{1,2,0:T(8,128)(2,1)}), bf16[4,128,128]{1,2,0:T(8,128)(2,1)S(1)}, u32[]{:S(2)}, u32[]{:S(2)}) async-start(bf16[4,128,128]{1,2,0:T(8,128)(2,1)} %bitcast.54), calls=%async_computation.1 | async-start | bytes 262144 | tf_op jit(solution)/shard_map/all_to_all | solution.py:176
  64.6 10.8 %all-to-all-start = ((bf16[4,128,256]{1,2,0:T(8,128)(2,1)}), bf16[4,128,256]{1,2,0:T(8,128)(2,1)S(1)}, u32[]{:S(2)}, u32[]{:S(2)}) async-start(bf16[4,128,256]{1,2,0:T(8,128)(2,1)} %bitcast.50), calls=%async_computation | async-start | bytes 524288 | tf_op jit(solution)/shard_map/all_to_all | solution.py:195
  79.4 11.5 %all-to-all-start.4 = ((bf16[4,128,256]{1,2,0:T(8,128)(2,1)}), bf16[4,128,256]{1,2,0:T(8,128)(2,1)S(1)}, u32[]{:S(2)}, u32[]{:S(2)}) async-start(bf16[4,128,256]{1,2,0:T(8,128)(2,1)} %copy.48), calls=%async_computation.4 | async-start | bytes 524288 | tf_op jit(solution)/shard_map/all_to_all | solution.py:227
  85.9 19.1 %copy-start.4 = (f32[128,3,8,64]{0,3,2,1:T(8,128)S(1)}, f32[128,3,8,64]{0,3,2,1:T(8,128)}, u32[]{:S(2)}) copy-start(f32[128,3,8,64]{0,3,2,1:T(8,128)} %copy-done.3) | copy-start | bytes 2359300
  90.8 10.2 %all-to-all-start.5 = ((f32[4,128,128]{1,2,0:T(8,128)}), f32[4,128,128]{1,2,0:T(8,128)S(1)}, u32[]{:S(2)}, u32[]{:S(2)}) async-start(f32[4,128,128]{1,2,0:T(8,128)} %copy.50), calls=%async_computation.5 | async-start | bytes 524288 | tf_op jit(solution)/shard_map/all_to_all | solution.py:218
  101.0 19.1 %all-to-all-start.2 = ((bf16[4,128,128]{1,2,0:T(8,128)(2,1)}), bf16[4,128,128]{1,2,0:T(8,128)(2,1)S(1)}, u32[]{:S(2)}, u32[]{:S(2)}) async-start(bf16[4,128,128]{1,2,0:T(8,128)(2,1)} %copy.42), calls=%async_computation.2 | async-start | bytes 262144 | tf_op jit(solution)/shard_map/all_to_all | solution.py:207
  105.0 104.8 %all-reduce.8.cloned.1.call-start = ((), (), s32[]{:S(2)}) async-start(), calls=%async_computation.9 | async-start | bytes 262144 | tf_op jit(solution)/shard_map/psum | solution.py:261
  108.5 11.6 %copy-start.5 = (bf16[512,1024]{1,0:T(8,128)(2,1)S(1)}, bf16[512,1024]{1,0:T(8,128)(2,1)}, u32[]{:S(2)}) copy-start(bf16[512,1024]{1,0:T(8,128)(2,1)} %all-gather.8.cloned.1.call-done) | copy-start | bytes 3145732
  108.5 11.6 %copy-start.64 = (f32[1,1,1024]{2,0,1:T(1,128)S(1)}, f32[1,1,1024]{2,0,1:T(1,128)}, u32[]{:S(2)}) copy-start(f32[1,1,1024]{2,0,1:T(1,128)} %copy-done.63) | copy-start | bytes 12292
  109.8 101.6 %collective-permute-start.3 = (bf16[1,1,8,16,1024]{4,3,2,1,0:T(8,128)(2,1)S(1)}, bf16[1,1,8,16,1024]{4,3,2,1,0:T(8,128)(2,1)S(1)}, u32[]{:S(2)}, u32[]{:S(2)}) collective-permute-start(bf16[1,1,8,16,1024]{4,3,2,1,0:T(8,128)(2,1)S(1)} %bitcast.244), channel_id=1, source_target_pairs={{4,0},{8,4},{12,8},{5,1},{9,5},{13,9},{6,2},{10,6},{14,10},{7,3},{... | collective-permute-start | bytes 786440 | tf_op jit(solution)/shard_map/ppermute | solution.py:19
  111.8 99.7 %collective-permute-start.2 = (bf16[1,1,8,16,1024]{4,3,2,1,0:T(8,128)(2,1)S(1)}, bf16[1,1,8,16,1024]{4,3,2,1,0:T(8,128)(2,1)S(1)}, u32[]{:S(2)}, u32[]{:S(2)}) collective-permute-start(bf16[1,1,8,16,1024]{4,3,2,1,0:T(8,128)(2,1)S(1)} %bitcast.245), channel_id=1, source_target_pairs={{0,4},{4,8},{8,12},{1,5},{5,9},{9,13},{2,6},{6,10},{10,14},{3,7},{... | collective-permute-start | bytes 786440 | tf_op jit(solution)/shard_map/ppermute | solution.py:18
  120.2 91.3 %copy-start.16 = (f32[1,1024]{1,0:T(1,128)S(1)}, f32[1,1024]{1,0:T(1,128)}, u32[]{:S(2)}) copy-start(f32[1,1024]{1,0:T(1,128)} %copy-done.15) | copy-start | bytes 12292
  120.2 91.3 %copy-start.18 = (f32[1,1024]{1,0:T(1,128)S(1)}, f32[1,1024]{1,0:T(1,128)}, u32[]{:S(2)}) copy-start(f32[1,1024]{1,0:T(1,128)} %copy-done.17) | copy-start | bytes 12292
  120.2 91.3 %copy-start.20 = (f32[1,1024]{1,0:T(1,128)S(1)}, f32[1,1024]{1,0:T(1,128)}, u32[]{:S(2)}) copy-start(f32[1,1024]{1,0:T(1,128)} %copy-done.19) | copy-start | bytes 12292
  120.2 91.3 %copy-start.22 = (f32[1,1024]{1,0:T(1,128)S(1)}, f32[1,1024]{1,0:T(1,128)}, u32[]{:S(2)}) copy-start(f32[1,1024]{1,0:T(1,128)} %copy-done.21) | copy-start | bytes 12292
  120.2 91.3 %copy-start.24 = (f32[1,1024]{1,0:T(1,128)S(1)}, f32[1,1024]{1,0:T(1,128)}, u32[]{:S(2)}) copy-start(f32[1,1024]{1,0:T(1,128)} %copy-done.23) | copy-start | bytes 12292
  120.2 91.3 %copy-start.26 = (f32[1,1024]{1,0:T(1,128)S(1)}, f32[1,1024]{1,0:T(1,128)}, u32[]{:S(2)}) copy-start(f32[1,1024]{1,0:T(1,128)} %copy-done.25) | copy-start | bytes 12292
  120.3 91.3 %copy-start.28 = (f32[1,1024]{1,0:T(1,128)S(1)}, f32[1,1024]{1,0:T(1,128)}, u32[]{:S(2)}) copy-start(f32[1,1024]{1,0:T(1,128)} %copy-done.27) | copy-start | bytes 12292
  120.3 91.3 %copy-start.30 = (f32[1,1024]{1,0:T(1,128)S(1)}, f32[1,1024]{1,0:T(1,128)}, u32[]{:S(2)}) copy-start(f32[1,1024]{1,0:T(1,128)} %copy-done.29) | copy-start | bytes 12292
  120.3 91.3 %copy-start.32 = (f32[1,1024]{1,0:T(1,128)S(1)}, f32[1,1024]{1,0:T(1,128)}, u32[]{:S(2)}) copy-start(f32[1,1024]{1,0:T(1,128)} %copy-done.31) | copy-start | bytes 12292
  120.3 91.3 %copy-start.34 = (f32[1,1024]{1,0:T(1,128)S(1)}, f32[1,1024]{1,0:T(1,128)}, u32[]{:S(2)}) copy-start(f32[1,1024]{1,0:T(1,128)} %copy-done.33) | copy-start | bytes 12292
  120.3 91.3 %copy-start.36 = (f32[1,1024]{1,0:T(1,128)S(1)}, f32[1,1024]{1,0:T(1,128)}, u32[]{:S(2)}) copy-start(f32[1,1024]{1,0:T(1,128)} %copy-done.35) | copy-start | bytes 12292
  120.3 91.3 %copy-start.38 = (f32[1,1024]{1,0:T(1,128)S(1)}, f32[1,1024]{1,0:T(1,128)}, u32[]{:S(2)}) copy-start(f32[1,1024]{1,0:T(1,128)} %copy-done.37) | copy-start | bytes 12292
  120.3 91.3 %copy-start.40 = (f32[1,1024]{1,0:T(1,128)S(1)}, f32[1,1024]{1,0:T(1,128)}, u32[]{:S(2)}) copy-start(f32[1,1024]{1,0:T(1,128)} %copy-done.39) | copy-start | bytes 12292
  120.3 91.3 %copy-start.42 = (f32[1,1024]{1,0:T(1,128)S(1)}, f32[1,1024]{1,0:T(1,128)}, u32[]{:S(2)}) copy-start(f32[1,1024]{1,0:T(1,128)} %copy-done.41) | copy-start | bytes 12292
  120.3 91.3 %copy-start.44 = (f32[1,1024]{1,0:T(1,128)S(1)}, f32[1,1024]{1,0:T(1,128)}, u32[]{:S(2)}) copy-start(f32[1,1024]{1,0:T(1,128)} %copy-done.43) | copy-start | bytes 12292
  120.3 91.3 %copy-start.46 = (f32[1,1024]{1,0:T(1,128)S(1)}, f32[1,1024]{1,0:T(1,128)}, u32[]{:S(2)}) copy-start(f32[1,1024]{1,0:T(1,128)} %copy-done.45) | copy-start | bytes 12292
  120.4 91.3 %copy-start.48 = (f32[1,1024]{1,0:T(1,128)S(1)}, f32[1,1024]{1,0:T(1,128)}, u32[]{:S(2)}) copy-start(f32[1,1024]{1,0:T(1,128)} %copy-done.47) | copy-start | bytes 12292
  120.4 91.3 %copy-start.50 = (f32[1,1024]{1,0:T(1,128)S(1)}, f32[1,1024]{1,0:T(1,128)}, u32[]{:S(2)}) copy-start(f32[1,1024]{1,0:T(1,128)} %copy-done.49) | copy-start | bytes 12292
  120.4 91.3 %copy-start.52 = (f32[1,1024]{1,0:T(1,128)S(1)}, f32[1,1024]{1,0:T(1,128)}, u32[]{:S(2)}) copy-start(f32[1,1024]{1,0:T(1,128)} %copy-done.51) | copy-start | bytes 12292
  120.4 91.3 %copy-start.54 = (f32[1,1024]{1,0:T(1,128)S(1)}, f32[1,1024]{1,0:T(1,128)}, u32[]{:S(2)}) copy-start(f32[1,1024]{1,0:T(1,128)} %copy-done.53) | copy-start | bytes 12292
  120.4 91.3 %copy-start.56 = (f32[1,1024]{1,0:T(1,128)S(1)}, f32[1,1024]{1,0:T(1,128)}, u32[]{:S(2)}) copy-start(f32[1,1024]{1,0:T(1,128)} %copy-done.55) | copy-start | bytes 12292
  120.4 91.3 %copy-start.58 = (f32[1,1024]{1,0:T(1,128)S(1)}, f32[1,1024]{1,0:T(1,128)}, u32[]{:S(2)}) copy-start(f32[1,1024]{1,0:T(1,128)} %copy-done.57) | copy-start | bytes 12292
  120.4 91.3 %copy-start.60 = (f32[1,1024]{1,0:T(1,128)S(1)}, f32[1,1024]{1,0:T(1,128)}, u32[]{:S(2)}) copy-start(f32[1,1024]{1,0:T(1,128)} %copy-done.59) | copy-start | bytes 12292
  120.4 91.3 %copy-start.62 = (f32[1,1024]{1,0:T(1,128)S(1)}, f32[1,1024]{1,0:T(1,128)}, u32[]{:S(2)}) copy-start(f32[1,1024]{1,0:T(1,128)} %copy-done.61) | copy-start | bytes 12292
  (19 other events, 84.6 us)
Sparse Core Ops, SparseCore 0:
  9.7 11.0 all-gather.3
  22.3 10.1 all-gather.7
  34.1 13.2 all-gather.5
  120.3 89.5 all-reduce.7
where the time goes:
time: 222 us; the launch traced here: 221 us
  waiting for transfers between devices  124 us (56%)
  starting transfers between devices  40 us (18%)
  local copies, waits for them, and re-layouts  17.4 us (8%)
  between operations  15.6 us (7%)
  other arithmetic  13.9 us (6%)
  matrix products  10.6 us (5%)
    psum x1, waiting for transfers between devices, shards(): grad_kernel = lax.psum(local_terms, ('seq', 'dp', 'fsdp')) * norm_factor  88.4 us
    ppermute x2, starting transfers between devices, padded_2(): before = lax.ppermute(last, axis, up)  7.59 us
    all_gather x1, waiting for transfers between devices, shards(): lax.all_gather(qkv_weight, 'fsdp', axis=0, tiled=True)  6.31 us
    all_to_all x1, waiting for transfers between devices, shards(): lax.all_to_all(dquery.reshape(seq_count, part_rows, group_width), 'seq',...  6.13 us
    all_to_all x1, waiting for transfers between devices, shards(): lax.all_to_all(copies.reshape(seq_count, row_count, 2 * group_width), 'se...  5.98 us
    unnamed x139, local copies, waits for them, and re-layouts  5.94 us
    all_to_all x1, starting transfers between devices, shards(): lax.all_to_all(grads_kv.reshape(seq_count, row_count, 2 * group_width).as...  5.23 us
    all_to_all x1, starting transfers between devices, shards(): lax.all_to_all(to_heads(grad_attn), 'seq', split_axis=0, concat_axis=0, t...  5.16 us
  transfers between devices with their start and end apart: 14, of which 9 were waited for; matrix products, arithmetic and copies ran while one was open for 13% of the time, Pallas kernels for 0%

commit v1 on v0

--- a/solution.py
+++ b/solution.py
@@ -258,7 +258,7 @@
     norm_factor = 1.0 / math.sqrt(
         lax.axis_size("dp") * lax.axis_size("fsdp") * seq_count * row_count
     )
-    grad_kernel = lax.psum(local_terms, ("seq", "dp", "fsdp")) * norm_factor
+    grad_kernel = jnp.sum(lax.all_gather(local_terms, ("seq", "dp", "fsdp")), axis=0) * norm_factor
     return (out_rows.reshape(tokens.shape), grad_tokens.reshape(tokens.shape), grad_kernel)
 
 

time: 222 us -> 166 us (0.75)
  the two profiles are of different devices: /device:TPU:8 before, /device:TPU:0 now
where the time goes in v1:
time: 166 us; the launch traced here: 165 us
  waiting for transfers between devices  66.6 us (40%)
  starting transfers between devices  36.4 us (22%)
  other arithmetic  18.1 us (11%)
  local copies, waits for them, and re-layouts  17.6 us (11%)
  between operations  15.8 us (10%)
  matrix products  10.6 us (6%)
    all_gather x1, waiting for transfers between devices, shards(): lax.all_gather(local_terms, ('seq', 'dp', 'fsdp'))  23.1 us
    ppermute x2, starting transfers between devices, padded_2(): before = lax.ppermute(last, axis, up)  9.52 us
    all_to_all x1, waiting for transfers between devices, shards(): lax.all_to_all(copies.reshape(seq_count, row_count, 2 * group_width), 'se...  7.8 us
    ppermute x2, waiting for transfers between devices, padded_2(): after = lax.ppermute(leading, axis, down)  7.08 us
    all_gather x1, waiting for transfers between devices, shards(): lax.all_gather(qkv_weight, 'fsdp', axis=0, tiled=True)  6.6 us
    all_to_all x1, waiting for transfers between devices, shards(): lax.all_to_all(dquery.reshape(seq_count, part_rows, group_width), 'seq',...  5.71 us
    all_to_all x1, starting transfers between devices, shards(): lax.all_to_all(to_heads(query_f.astype(jnp.bfloat16)), 'seq', split_axis=...  4.86 us
    all_to_all x1, starting transfers between devices, shards(): lax.all_to_all(to_heads(grad_attn), 'seq', split_axis=0, concat_axis=0, t...  4.85 us
  transfers between devices with their start and end apart: 14, of which 12 were waited for; matrix products, arithmetic and copies ran while one was open for 15% of the time, Pallas kernels for 0%

profile of v1, /device:TPU:0, one launch (start us, length us, event | category | flops | bytes accessed | tf_op | source)
XLA Modules:
  0.0 165.2 jit_solution(7648555025534904395)
XLA Ops:
  7.2 2.3 %copy.35 = bf16[128,3072]{0,1:T(8,128)(2,1)} copy(bf16[128,3072]{1,0:T(8,128)(2,1)} %param.11) | data formatting | bytes 1572864 | tf_op args[3]
  9.6 0.7 all-gather.11.cloned.1.call-update
  10.4 0.7 all-gather.9.cloned.1.call-update
  11.1 4.9 %collective-permute-start = (bf16[1,1,8,16,1024]{4,3,2,1,0:T(8,128)(2,1)S(1)}, bf16[1,1,8,16,1024]{4,3,2,1,0:T(8,128)(2,1)S(1)}, u32[]{:S(2)}, u32[]{:S(2)}) collective-permute-start(bf16[1,1,8,16,1024]{4,3,2,1,0:T(8,128)(2,1)S(1)} %copy-done.5), channel_id=1, source_target_pairs={{0,4},{4,8},{8,12},{1,5},{5,9},{9,13},{2,6},{6,10},{10,14},{3,7},{... | collective-permute-start | bytes 786440 | tf_op jit(solution)/shard_map/ppermute | solution.py:18
  16.0 1.3 collective-permute-start.1
  18.5 3.1 %collective-permute-done = bf16[1,1,8,16,1024]{4,3,2,1,0:T(8,128)(2,1)S(1)} collective-permute-done((bf16[1,1,8,16,1024]{4,3,2,1,0:T(8,128)(2,1)S(1)}, bf16[1,1,8,16,1024]{4,3,2,1,0:T(8,128)(2,1)S(1)}, u32[]{:S(2)}, u32[]{:S(2)}) %collective-permute-start) | collective-permute-done | bytes 262176 | tf_op jit(solution)/shard_map/ppermute | solution.py:18
  21.6 4.1 %collective-permute-done.1 = bf16[1,1,8,16,1024]{4,3,2,1,0:T(8,128)(2,1)S(1)} collective-permute-done((bf16[1,1,8,16,1024]{4,3,2,1,0:T(8,128)(2,1)S(1)}, bf16[1,1,8,16,1024]{4,3,2,1,0:T(8,128)(2,1)S(1)}, u32[]{:S(2)}, u32[]{:S(2)}) %collective-permute-start.1) | collective-permute-done | bytes 262176 | tf_op jit(solution)/shard_map/ppermute | solution.py:19
  25.8 0.9 copy-done.1
  26.7 2.7 %convert_reduce_fusion = (f32[8,16]{1,0:T(8,128)S(1)}, bf16[1,8,16,1024]{3,2,1,0:T(8,128)(2,1)S(1)}) fusion(f32[1024]{0:T(1024)S(1)} %bitcast.275, f32[1024]{0:T(1024)S(1)} %bitcast.277, f32[1024]{0:T(1024)S(1)} %bitcast.281, f32[1024]{0:T(1024)S(1)} %bitcast.283, bf16[1,1,8,16,1024]{4,3,2,1,0:T(8,128)(2,1)S(1)} %collective-permute-done.1, ...), kind=kLoop, calls=%fused_computation.221 | loop fusion | flops 11009920 | bytes 1946112 | tf_op jit(solution)/shard_map/reduce_sum | solution.py:72
  29.9 0.6 multiply_add_fusion.1
  30.5 2.0 %fusion.103 = f32[1,3,1024]{2,0,1:T(1,128)S(1)} fusion(bf16[256,1,1]{0,1,2:T(2,128)(2,1)S(1)} %reshape.540, bf16[3,1024,256]{2,1,0:T(8,128)(2,1)} %bitcast.251), kind=kOutput, calls=%fused_computation.254 | convolution fusion | flops 1572864 | bytes 1585664 | tf_op jit(solution)/shard_map/dot_general | solution.py:34
  32.6 1.3 all-gather.11.cloned.1.call-done
  34.0 1.7 %convolution_convert_fusion.2 = bf16[128,512]{1,0:T(8,128)(2,1)S(1)} fusion(bf16[512,1024]{1,0:T(8,128)(2,1)} %all-gather.11.cloned.1.call-done, bf16[128,1024]{1,0:T(8,128)(2,1)S(1)} %bitcast.255, f32[1024]{0:T(1024)S(1)} %bitcast.317), kind=kOutput, calls=%fused_computation.88 | convolution fusion | flops 134676480 | bytes 1445888 | tf_op jit(solution)/shard_map/dot_general | solution.py:163
  35.7 0.8 copy.58
  36.4 4.9 %all-to-all-start.3 = ((bf16[4,128,128]{1,2,0:T(8,128)(2,1)}), bf16[4,128,128]{1,2,0:T(8,128)(2,1)S(1)}, u32[]{:S(2)}, u32[]{:S(2)}) async-start(bf16[4,128,128]{1,2,0:T(8,128)(2,1)} %bitcast.65), calls=%async_computation.3 | async-start | bytes 262144 | tf_op jit(solution)/shard_map/all_to_all | solution.py:179
  41.3 0.9 add_convert_fusion.1
  42.2 6.6 %all-gather.9.cloned.1.call-done = bf16[1024,1536]{1,0:T(8,128)(2,1)} async-done(((bf16[512,1536]{1,0:T(8,128)(2,1)}), bf16[1024,1536]{1,0:T(8,128)(2,1)}) %all-gather.9.cloned.1.call-update) | async-done | bytes 3145744 | tf_op jit(solution)/shard_map/all_gather | solution.py:132
  48.8 3.2 %copy.36 = bf16[1536,1024]{1,0:T(8,128)(2,1)S(1)} copy(bf16[1536,1024]{0,1:T(8,128)(2,1)} %bitcast.243) | data formatting | bytes 6291456 | tf_op jit(solution)/shard_map/dot_general | solution.py:159
  52.0 1.9 %fusion.104 = f32[128,3,8,64]{0,3,2,1:T(8,128)S(1)} fusion(bf16[128,1024,1,1]{1,0,3,2:T(8,128)(2,1)} %bitcast.254, bf16[3,8,64,1024]{3,2,1,0:T(8,128)(2,1)S(1)} %bitcast.244), kind=kOutput, calls=%fused_computation.255 | convolution fusion | flops 402653184 | bytes 4194304 | tf_op jit(solution)/shard_map/dot_general | solution.py:159
  54.0 0.8 copy-done.3
  54.9 0.7 fusion.98
  55.6 4.9 %all-to-all-start.1 = ((bf16[4,128,128]{1,2,0:T(8,128)(2,1)}), bf16[4,128,128]{1,2,0:T(8,128)(2,1)S(1)}, u32[]{:S(2)}, u32[]{:S(2)}) async-start(bf16[4,128,128]{1,2,0:T(8,128)(2,1)} %bitcast.54), calls=%async_computation.1 | async-start | bytes 262144 | tf_op jit(solution)/shard_map/all_to_all | solution.py:176
  60.4 1.0 slice.712
  61.4 0.7 pad_maximum_fusion
  62.1 4.7 %all-to-all-done.1 = bf16[4,128,128]{1,2,0:T(8,128)(2,1)S(1)} async-done(((bf16[4,128,128]{1,2,0:T(8,128)(2,1)}), bf16[4,128,128]{1,2,0:T(8,128)(2,1)S(1)}, u32[]{:S(2)}, u32[]{:S(2)}) %all-to-all-start.1) | async-done | bytes 131104 | tf_op jit(solution)/shard_map/all_to_all | solution.py:176
  66.8 3.4 %all-to-all-start = ((bf16[4,128,256]{1,2,0:T(8,128)(2,1)}), bf16[4,128,256]{1,2,0:T(8,128)(2,1)S(1)}, u32[]{:S(2)}, u32[]{:S(2)}) async-start(bf16[4,128,256]{1,2,0:T(8,128)(2,1)} %bitcast.50), calls=%async_computation | async-start | bytes 524288 | tf_op jit(solution)/shard_map/all_to_all | solution.py:195
  70.6 7.8 %all-to-all-done = bf16[4,128,256]{1,2,0:T(8,128)(2,1)S(1)} async-done(((bf16[4,128,256]{1,2,0:T(8,128)(2,1)}), bf16[4,128,256]{1,2,0:T(8,128)(2,1)S(1)}, u32[]{:S(2)}, u32[]{:S(2)}) %all-to-all-start) | async-done | bytes 262176 | tf_op jit(solution)/shard_map/all_to_all | solution.py:195
  78.4 0.2 copy.39
  78.7 0.5 fusion.1
  79.2 0.3 fusion.7
  79.6 0.4 fusion.6
  80.0 0.3 multiply_reduce_fusion.4
  80.3 0.7 multiply_convert_fusion
  81.0 0.4 fusion.5
  81.6 0.7 copy.48
  82.3 3.4 %all-to-all-start.4 = ((bf16[4,128,256]{1,2,0:T(8,128)(2,1)}), bf16[4,128,256]{1,2,0:T(8,128)(2,1)S(1)}, u32[]{:S(2)}, u32[]{:S(2)}) async-start(bf16[4,128,256]{1,2,0:T(8,128)(2,1)} %copy.48), calls=%async_computation.4 | async-start | bytes 524288 | tf_op jit(solution)/shard_map/all_to_all | solution.py:227
  85.8 0.6 div.54
  86.4 0.6 add.273
  86.9 0.3 convolution_bitcast_fusion
  87.3 0.7 copy.50
  88.1 4.4 %all-to-all-done.4 = bf16[4,128,256]{1,2,0:T(8,128)(2,1)S(1)} async-done(((bf16[4,128,256]{1,2,0:T(8,128)(2,1)}), bf16[4,128,256]{1,2,0:T(8,128)(2,1)S(1)}, u32[]{:S(2)}, u32[]{:S(2)}) %all-to-all-start.4) | async-done | bytes 262176 | tf_op jit(solution)/shard_map/all_to_all | solution.py:227
  92.5 4.0 %all-to-all-start.5 = ((f32[4,128,128]{1,2,0:T(8,128)}), f32[4,128,128]{1,2,0:T(8,128)}, u32[]{:S(2)}, u32[]{:S(2)}) async-start(f32[4,128,128]{1,2,0:T(8,128)} %copy.50), calls=%async_computation.5 | async-start | bytes 524288 | tf_op jit(solution)/shard_map/all_to_all | solution.py:218
  96.5 0.2 all-gather.13.cloned.1.call-start
  96.8 0.8 fusion.97
  97.7 5.7 %all-to-all-done.5 = f32[4,128,128]{1,2,0:T(8,128)} async-done(((f32[4,128,128]{1,2,0:T(8,128)}), f32[4,128,128]{1,2,0:T(8,128)}, u32[]{:S(2)}, u32[]{:S(2)}) %all-to-all-start.5) | async-done | bytes 262176 | tf_op jit(solution)/shard_map/all_to_all | solution.py:218
  103.4 1.3 multiply_reduce_fusion.1
  104.7 1.3 add_add_fusion.1
  106.0 1.0 add_convert_fusion
  107.1 1.2 multiply_reduce_fusion
  108.4 0.3 fusion.94
  108.7 1.3 fusion.75
  110.0 1.6 fusion.76
  111.6 2.6 %stack.130 = f32[27,1024]{1,0:T(8,128)} concatenate(f32[1,1024]{1,0:T(1,128)S(1)} %bitcast.331, f32[1,1024]{1,0:T(1,128)S(1)} %bitcast.332, f32[1,1024]{1,0:T(1,128)S(1)} %bitcast.333, f32[1,1024]{1,0:T(1,128)S(1)} %bitcast.334, f32[1,1024]{1,0:T(1,128)S(1)} %bitcast.329, f32[1,1024]{1,0:T(1,128)S(1)} %bitcast.335, f32[1,1024]{1,0:T(1,128)S(1)} %bitcast.336, ...), dimensions={0} | concatenate | bytes 221184 | tf_op jit(solution)/shard_map/stack | solution.py:68
  114.6 0.7 copy.42
  115.2 3.4 %all-to-all-start.2 = ((bf16[4,128,128]{1,2,0:T(8,128)(2,1)}), bf16[4,128,128]{1,2,0:T(8,128)(2,1)S(1)}, u32[]{:S(2)}, u32[]{:S(2)}) async-start(bf16[4,128,128]{1,2,0:T(8,128)(2,1)} %copy.42), calls=%async_computation.2 | async-start | bytes 262144 | tf_op jit(solution)/shard_map/all_to_all | solution.py:207
  118.7 1.3 collective-permute-start.3
  119.9 4.6 %collective-permute-start.2 = (bf16[1,1,8,16,1024]{4,3,2,1,0:T(8,128)(2,1)S(1)}, bf16[1,1,8,16,1024]{4,3,2,1,0:T(8,128)(2,1)S(1)}, u32[]{:S(2)}, u32[]{:S(2)}) collective-permute-start(bf16[1,1,8,16,1024]{4,3,2,1,0:T(8,128)(2,1)S(1)} %bitcast.246), channel_id=1, source_target_pairs={{0,4},{4,8},{8,12},{1,5},{5,9},{9,13},{2,6},{6,10},{10,14},{3,7},{... | collective-permute-start | bytes 786440 | tf_op jit(solution)/shard_map/ppermute | solution.py:18
  124.7 1.0 fusion.3
  125.7 3.0 %collective-permute-done.3 = bf16[1,1,8,16,1024]{4,3,2,1,0:T(8,128)(2,1)S(1)} collective-permute-done((bf16[1,1,8,16,1024]{4,3,2,1,0:T(8,128)(2,1)S(1)}, bf16[1,1,8,16,1024]{4,3,2,1,0:T(8,128)(2,1)S(1)}, u32[]{:S(2)}, u32[]{:S(2)}) %collective-permute-start.3) | collective-permute-done | bytes 262176 | tf_op jit(solution)/shard_map/ppermute | solution.py:19
  128.7 1.2 collective-permute-done.2
  130.2 2.9 %fusion.90 = bf16[1,1,8,16,1024]{4,3,2,1,0:T(8,128)(2,1)} fusion(bf16[3,8,16,1024]{3,2,1,0:T(8,128)(2,1)S(1)} %maximum_bitcast_fusion.1, f32[1024]{0:T(1024)S(1)} %bitcast.280, f32[1024]{0:T(1024)S(1)} %bitcast.264, f32[1024]{0:T(1024)S(1)} %bitcast.274, f32[1024]{0:T(1024)S(1)} %bitcast.272, bf16[1,1,8,16,1024]{4,3,2,1,0:T(8,128)(2,1)S(1)} %collective-permute-done.3, ...), kind=kLoop, calls=%fused_computation.227 | loop fusion | flops 10747904 | bytes 1945600 | tf_op jit(solution)/shard_map/reshape | solution.py:262
  133.2 23.1 %all-gather.13.cloned.1.call-done = f32[16,27,1024]{2,1,0:T(8,128)} async-done(((f32[1,27,1024]{2,1,0:T(8,128)}), f32[16,27,1024]{2,1,0:T(8,128)}) %all-gather.13.cloned.1.call-update) | async-done | bytes 1769488 | tf_op jit(solution)/shard_map/all_gather | solution.py:261
  156.3 1.7 %reduce_sum.389 = f32[27,1024]{1,0:T(8,128)S(1)} reduce(f32[16,27,1024]{2,1,0:T(8,128)} %all-gather.13.cloned.1.call-done, f32[]{:T(128)} %constant.17.clone.1), dimensions={0}, to_apply=%region_35.36 | reduce | flops 414720 | bytes 1880068 | tf_op jit(solution)/shard_map/reduce_sum | solution.py:261
  158.0 0.7 broadcast_multiply_fusion
  (190 shorter events, 2.0 us)
Async XLA Ops:
  7.2 23.3 %all-gather.7.cloned.1.call-start = ((), (), s32[]{:S(2)}) async-start(), calls=%async_computation.6 | async-start | bytes 2359296 | tf_op jit(solution)/shard_map/all_gather | solution.py:134
  9.6 24.4 %all-gather.11.cloned.1.call-start = ((), (), s32[]{:S(2)}) async-start(), calls=%async_computation.8 | async-start | bytes 1572864 | tf_op jit(solution)/shard_map/all_gather | solution.py:133
  10.4 38.5 %all-gather.9.cloned.1.call-start = ((), (), s32[]{:S(2)}) async-start(), calls=%async_computation.7 | async-start | bytes 4718592 | tf_op jit(solution)/shard_map/all_gather | solution.py:132
  11.1 10.5 %collective-permute-start = (bf16[1,1,8,16,1024]{4,3,2,1,0:T(8,128)(2,1)S(1)}, bf16[1,1,8,16,1024]{4,3,2,1,0:T(8,128)(2,1)S(1)}, u32[]{:S(2)}, u32[]{:S(2)}) collective-permute-start(bf16[1,1,8,16,1024]{4,3,2,1,0:T(8,128)(2,1)S(1)} %copy-done.5), channel_id=1, source_target_pairs={{0,4},{4,8},{8,12},{1,5},{5,9},{9,13},{2,6},{6,10},{10,14},{3,7},{... | collective-permute-start | bytes 786440 | tf_op jit(solution)/shard_map/ppermute | solution.py:18
  16.0 9.7 %collective-permute-start.1 = (bf16[1,1,8,16,1024]{4,3,2,1,0:T(8,128)(2,1)S(1)}, bf16[1,1,8,16,1024]{4,3,2,1,0:T(8,128)(2,1)S(1)}, u32[]{:S(2)}, u32[]{:S(2)}) collective-permute-start(bf16[1,1,8,16,1024]{4,3,2,1,0:T(8,128)(2,1)S(1)} %copy-done.5), channel_id=1, source_target_pairs={{4,0},{8,4},{12,8},{5,1},{9,5},{13,9},{6,2},{10,6},{14,10},{7,3},{... | collective-permute-start | bytes 786440 | tf_op jit(solution)/shard_map/ppermute | solution.py:19
  18.1 11.6 %copy-start.20 = (f32[1,1024]{1,0:T(1,128)}, f32[1,1024]{1,0:T(1,128)S(1)}, u32[]{:S(2)}) copy-start(f32[1,1024]{1,0:T(1,128)S(1)} %get-tuple-element.85) | copy-start | bytes 12292
  18.1 11.6 %copy-start.22 = (f32[1,1024]{1,0:T(1,128)}, f32[1,1024]{1,0:T(1,128)S(1)}, u32[]{:S(2)}) copy-start(f32[1,1024]{1,0:T(1,128)S(1)} %get-tuple-element.86) | copy-start | bytes 12292
  18.1 11.6 %copy-start.24 = (f32[1,1024]{1,0:T(1,128)}, f32[1,1024]{1,0:T(1,128)S(1)}, u32[]{:S(2)}) copy-start(f32[1,1024]{1,0:T(1,128)S(1)} %get-tuple-element.87) | copy-start | bytes 12292
  18.1 11.6 %copy-start.26 = (f32[1,1024]{1,0:T(1,128)}, f32[1,1024]{1,0:T(1,128)S(1)}, u32[]{:S(2)}) copy-start(f32[1,1024]{1,0:T(1,128)S(1)} %get-tuple-element.88) | copy-start | bytes 12292
  18.2 11.6 %copy-start.28 = (f32[1,1024]{1,0:T(1,128)}, f32[1,1024]{1,0:T(1,128)S(1)}, u32[]{:S(2)}) copy-start(f32[1,1024]{1,0:T(1,128)S(1)} %get-tuple-element.89) | copy-start | bytes 12292
  18.2 11.6 %copy-start.30 = (f32[1,1024]{1,0:T(1,128)}, f32[1,1024]{1,0:T(1,128)S(1)}, u32[]{:S(2)}) copy-start(f32[1,1024]{1,0:T(1,128)S(1)} %get-tuple-element.90) | copy-start | bytes 12292
  18.3 11.5 %copy-start.32 = (f32[1,1024]{1,0:T(1,128)}, f32[1,1024]{1,0:T(1,128)S(1)}, u32[]{:S(2)}) copy-start(f32[1,1024]{1,0:T(1,128)S(1)} %get-tuple-element.64) | copy-start | bytes 12292
  18.3 11.5 %copy-start.34 = (f32[1,1024]{1,0:T(1,128)}, f32[1,1024]{1,0:T(1,128)S(1)}, u32[]{:S(2)}) copy-start(f32[1,1024]{1,0:T(1,128)S(1)} %get-tuple-element.65) | copy-start | bytes 12292
  18.3 11.5 %copy-start.36 = (f32[1,1024]{1,0:T(1,128)}, f32[1,1024]{1,0:T(1,128)S(1)}, u32[]{:S(2)}) copy-start(f32[1,1024]{1,0:T(1,128)S(1)} %get-tuple-element.66) | copy-start | bytes 12292
  18.3 11.5 %copy-start.38 = (f32[1,1024]{1,0:T(1,128)}, f32[1,1024]{1,0:T(1,128)S(1)}, u32[]{:S(2)}) copy-start(f32[1,1024]{1,0:T(1,128)S(1)} %get-tuple-element.67) | copy-start | bytes 12292
  18.3 11.5 %copy-start.40 = (f32[1,1024]{1,0:T(1,128)}, f32[1,1024]{1,0:T(1,128)S(1)}, u32[]{:S(2)}) copy-start(f32[1,1024]{1,0:T(1,128)S(1)} %get-tuple-element.68) | copy-start | bytes 12292
  18.3 11.5 %copy-start.42 = (f32[1,1024]{1,0:T(1,128)}, f32[1,1024]{1,0:T(1,128)S(1)}, u32[]{:S(2)}) copy-start(f32[1,1024]{1,0:T(1,128)S(1)} %get-tuple-element.69) | copy-start | bytes 12292
  18.3 11.5 %copy-start.44 = (f32[1,1024]{1,0:T(1,128)}, f32[1,1024]{1,0:T(1,128)S(1)}, u32[]{:S(2)}) copy-start(f32[1,1024]{1,0:T(1,128)S(1)} %get-tuple-element.70) | copy-start | bytes 12292
  18.3 11.5 %copy-start.46 = (f32[1,1024]{1,0:T(1,128)}, f32[1,1024]{1,0:T(1,128)S(1)}, u32[]{:S(2)}) copy-start(f32[1,1024]{1,0:T(1,128)S(1)} %get-tuple-element.71) | copy-start | bytes 12292
  18.3 11.5 %copy-start.48 = (f32[1,1024]{1,0:T(1,128)}, f32[1,1024]{1,0:T(1,128)S(1)}, u32[]{:S(2)}) copy-start(f32[1,1024]{1,0:T(1,128)S(1)} %get-tuple-element.72) | copy-start | bytes 12292
  18.4 11.5 %copy-start.50 = (f32[1,1024]{1,0:T(1,128)}, f32[1,1024]{1,0:T(1,128)S(1)}, u32[]{:S(2)}) copy-start(f32[1,1024]{1,0:T(1,128)S(1)} %get-tuple-element.73) | copy-start | bytes 12292
  18.4 11.5 %copy-start.52 = (f32[1,1024]{1,0:T(1,128)}, f32[1,1024]{1,0:T(1,128)S(1)}, u32[]{:S(2)}) copy-start(f32[1,1024]{1,0:T(1,128)S(1)} %get-tuple-element.74) | copy-start | bytes 12292
  18.4 11.5 %copy-start.54 = (f32[1,1024]{1,0:T(1,128)}, f32[1,1024]{1,0:T(1,128)S(1)}, u32[]{:S(2)}) copy-start(f32[1,1024]{1,0:T(1,128)S(1)} %get-tuple-element.75) | copy-start | bytes 12292
  29.5 12.8 %copy-start.14 = (f32[8,16]{1,0:T(8,128)}, f32[8,16]{1,0:T(8,128)S(1)}, u32[]{:S(2)}) copy-start(f32[8,16]{1,0:T(8,128)S(1)} %broadcast_multiply_fusion.1) | copy-start | bytes 1540
  32.6 16.2 %copy-start.70 = (f32[1,1,1024]{2,0,1:T(1,128)}, f32[1,1,1024]{2,0,1:T(1,128)S(1)}, u32[]{:S(2)}) copy-start(f32[1,1,1024]{2,0,1:T(1,128)S(1)} %get-tuple-element.91) | copy-start | bytes 12292
  32.6 16.2 %copy-start.72 = (f32[1,1,1024]{2,0,1:T(1,128)}, f32[1,1,1024]{2,0,1:T(1,128)S(1)}, u32[]{:S(2)}) copy-start(f32[1,1,1024]{2,0,1:T(1,128)S(1)} %get-tuple-element.93) | copy-start | bytes 12292
  36.4 19.2 %all-to-all-start.3 = ((bf16[4,128,128]{1,2,0:T(8,128)(2,1)}), bf16[4,128,128]{1,2,0:T(8,128)(2,1)S(1)}, u32[]{:S(2)}, u32[]{:S(2)}) async-start(bf16[4,128,128]{1,2,0:T(8,128)(2,1)} %bitcast.65), calls=%async_computation.3 | async-start | bytes 262144 | tf_op jit(solution)/shard_map/all_to_all | solution.py:179
  55.6 11.2 %all-to-all-start.1 = ((bf16[4,128,128]{1,2,0:T(8,128)(2,1)}), bf16[4,128,128]{1,2,0:T(8,128)(2,1)S(1)}, u32[]{:S(2)}, u32[]{:S(2)}) async-start(bf16[4,128,128]{1,2,0:T(8,128)(2,1)} %bitcast.54), calls=%async_computation.1 | async-start | bytes 262144 | tf_op jit(solution)/shard_map/all_to_all | solution.py:176
  66.8 11.6 %all-to-all-start = ((bf16[4,128,256]{1,2,0:T(8,128)(2,1)}), bf16[4,128,256]{1,2,0:T(8,128)(2,1)S(1)}, u32[]{:S(2)}, u32[]{:S(2)}) async-start(bf16[4,128,256]{1,2,0:T(8,128)(2,1)} %bitcast.50), calls=%async_computation | async-start | bytes 524288 | tf_op jit(solution)/shard_map/all_to_all | solution.py:195
  82.3 10.2 %all-to-all-start.4 = ((bf16[4,128,256]{1,2,0:T(8,128)(2,1)}), bf16[4,128,256]{1,2,0:T(8,128)(2,1)S(1)}, u32[]{:S(2)}, u32[]{:S(2)}) async-start(bf16[4,128,256]{1,2,0:T(8,128)(2,1)} %copy.48), calls=%async_computation.4 | async-start | bytes 524288 | tf_op jit(solution)/shard_map/all_to_all | solution.py:227
  92.5 10.9 %all-to-all-start.5 = ((f32[4,128,128]{1,2,0:T(8,128)}), f32[4,128,128]{1,2,0:T(8,128)}, u32[]{:S(2)}, u32[]{:S(2)}) async-start(f32[4,128,128]{1,2,0:T(8,128)} %copy.50), calls=%async_computation.5 | async-start | bytes 524288 | tf_op jit(solution)/shard_map/all_to_all | solution.py:218
  96.5 59.7 %all-gather.13.cloned.1.call-start = ((), (), s32[]{:S(2)}) async-start(), calls=%async_computation.9 | async-start | bytes 2228224 | tf_op jit(solution)/shard_map/all_gather | solution.py:261
  108.7 16.0 %copy-start.4 = (bf16[512,1024]{1,0:T(8,128)(2,1)S(1)}, bf16[512,1024]{1,0:T(8,128)(2,1)}, u32[]{:S(2)}) copy-start(bf16[512,1024]{1,0:T(8,128)(2,1)} %all-gather.11.cloned.1.call-done) | copy-start | bytes 3145732
  108.7 16.0 %copy-start.71 = (f32[1,1,1024]{2,0,1:T(1,128)S(1)}, f32[1,1,1024]{2,0,1:T(1,128)}, u32[]{:S(2)}) copy-start(f32[1,1,1024]{2,0,1:T(1,128)} %copy-done.70) | copy-start | bytes 12292
  114.3 15.7 %copy-start.17 = (f32[1,1024]{1,0:T(1,128)S(1)}, f32[1,1024]{1,0:T(1,128)}, u32[]{:S(2)}) copy-start(f32[1,1024]{1,0:T(1,128)} %copy-done.16) | copy-start | bytes 12292
  114.3 15.7 %copy-start.19 = (f32[1,1024]{1,0:T(1,128)S(1)}, f32[1,1024]{1,0:T(1,128)}, u32[]{:S(2)}) copy-start(f32[1,1024]{1,0:T(1,128)} %copy-done.18) | copy-start | bytes 12292
  114.3 15.7 %copy-start.21 = (f32[1,1024]{1,0:T(1,128)S(1)}, f32[1,1024]{1,0:T(1,128)}, u32[]{:S(2)}) copy-start(f32[1,1024]{1,0:T(1,128)} %copy-done.20) | copy-start | bytes 12292
  114.3 15.7 %copy-start.23 = (f32[1,1024]{1,0:T(1,128)S(1)}, f32[1,1024]{1,0:T(1,128)}, u32[]{:S(2)}) copy-start(f32[1,1024]{1,0:T(1,128)} %copy-done.22) | copy-start | bytes 12292
  114.3 15.7 %copy-start.25 = (f32[1,1024]{1,0:T(1,128)S(1)}, f32[1,1024]{1,0:T(1,128)}, u32[]{:S(2)}) copy-start(f32[1,1024]{1,0:T(1,128)} %copy-done.24) | copy-start | bytes 12292
  114.3 15.7 %copy-start.27 = (f32[1,1024]{1,0:T(1,128)S(1)}, f32[1,1024]{1,0:T(1,128)}, u32[]{:S(2)}) copy-start(f32[1,1024]{1,0:T(1,128)} %copy-done.26) | copy-start | bytes 12292
  114.3 15.7 %copy-start.29 = (f32[1,1024]{1,0:T(1,128)S(1)}, f32[1,1024]{1,0:T(1,128)}, u32[]{:S(2)}) copy-start(f32[1,1024]{1,0:T(1,128)} %copy-done.28) | copy-start | bytes 12292
  114.3 15.7 %copy-start.31 = (f32[1,1024]{1,0:T(1,128)S(1)}, f32[1,1024]{1,0:T(1,128)}, u32[]{:S(2)}) copy-start(f32[1,1024]{1,0:T(1,128)} %copy-done.30) | copy-start | bytes 12292
  114.3 15.7 %copy-start.33 = (f32[1,1024]{1,0:T(1,128)S(1)}, f32[1,1024]{1,0:T(1,128)}, u32[]{:S(2)}) copy-start(f32[1,1024]{1,0:T(1,128)} %copy-done.32) | copy-start | bytes 12292
  114.3 15.7 %copy-start.35 = (f32[1,1024]{1,0:T(1,128)S(1)}, f32[1,1024]{1,0:T(1,128)}, u32[]{:S(2)}) copy-start(f32[1,1024]{1,0:T(1,128)} %copy-done.34) | copy-start | bytes 12292
  114.3 15.7 %copy-start.37 = (f32[1,1024]{1,0:T(1,128)S(1)}, f32[1,1024]{1,0:T(1,128)}, u32[]{:S(2)}) copy-start(f32[1,1024]{1,0:T(1,128)} %copy-done.36) | copy-start | bytes 12292
  114.3 15.7 %copy-start.39 = (f32[1,1024]{1,0:T(1,128)S(1)}, f32[1,1024]{1,0:T(1,128)}, u32[]{:S(2)}) copy-start(f32[1,1024]{1,0:T(1,128)} %copy-done.38) | copy-start | bytes 12292
  114.3 15.7 %copy-start.41 = (f32[1,1024]{1,0:T(1,128)S(1)}, f32[1,1024]{1,0:T(1,128)}, u32[]{:S(2)}) copy-start(f32[1,1024]{1,0:T(1,128)} %copy-done.40) | copy-start | bytes 12292
  114.4 15.7 %copy-start.43 = (f32[1,1024]{1,0:T(1,128)S(1)}, f32[1,1024]{1,0:T(1,128)}, u32[]{:S(2)}) copy-start(f32[1,1024]{1,0:T(1,128)} %copy-done.42) | copy-start | bytes 12292
  114.4 15.7 %copy-start.45 = (f32[1,1024]{1,0:T(1,128)S(1)}, f32[1,1024]{1,0:T(1,128)}, u32[]{:S(2)}) copy-start(f32[1,1024]{1,0:T(1,128)} %copy-done.44) | copy-start | bytes 12292
  114.4 15.7 %copy-start.47 = (f32[1,1024]{1,0:T(1,128)S(1)}, f32[1,1024]{1,0:T(1,128)}, u32[]{:S(2)}) copy-start(f32[1,1024]{1,0:T(1,128)} %copy-done.46) | copy-start | bytes 12292
  114.4 15.7 %copy-start.49 = (f32[1,1024]{1,0:T(1,128)S(1)}, f32[1,1024]{1,0:T(1,128)}, u32[]{:S(2)}) copy-start(f32[1,1024]{1,0:T(1,128)} %copy-done.48) | copy-start | bytes 12292
  114.4 15.7 %copy-start.51 = (f32[1,1024]{1,0:T(1,128)S(1)}, f32[1,1024]{1,0:T(1,128)}, u32[]{:S(2)}) copy-start(f32[1,1024]{1,0:T(1,128)} %copy-done.50) | copy-start | bytes 12292
  114.4 15.7 %copy-start.53 = (f32[1,1024]{1,0:T(1,128)S(1)}, f32[1,1024]{1,0:T(1,128)}, u32[]{:S(2)}) copy-start(f32[1,1024]{1,0:T(1,128)} %copy-done.52) | copy-start | bytes 12292
  114.4 15.7 %copy-start.55 = (f32[1,1024]{1,0:T(1,128)S(1)}, f32[1,1024]{1,0:T(1,128)}, u32[]{:S(2)}) copy-start(f32[1,1024]{1,0:T(1,128)} %copy-done.54) | copy-start | bytes 12292
  114.4 15.7 %copy-start.57 = (f32[1,1024]{1,0:T(1,128)S(1)}, f32[1,1024]{1,0:T(1,128)}, u32[]{:S(2)}) copy-start(f32[1,1024]{1,0:T(1,128)} %copy-done.56) | copy-start | bytes 12292
  114.4 15.7 %copy-start.59 = (f32[1,1024]{1,0:T(1,128)S(1)}, f32[1,1024]{1,0:T(1,128)}, u32[]{:S(2)}) copy-start(f32[1,1024]{1,0:T(1,128)} %copy-done.58) | copy-start | bytes 12292
  114.4 15.7 %copy-start.61 = (f32[1,1024]{1,0:T(1,128)S(1)}, f32[1,1024]{1,0:T(1,128)}, u32[]{:S(2)}) copy-start(f32[1,1024]{1,0:T(1,128)} %copy-done.60) | copy-start | bytes 12292
  114.5 15.7 %copy-start.63 = (f32[1,1024]{1,0:T(1,128)S(1)}, f32[1,1024]{1,0:T(1,128)}, u32[]{:S(2)}) copy-start(f32[1,1024]{1,0:T(1,128)} %copy-done.62) | copy-start | bytes 12292
  114.5 15.7 %copy-start.65 = (f32[1,1024]{1,0:T(1,128)S(1)}, f32[1,1024]{1,0:T(1,128)}, u32[]{:S(2)}) copy-start(f32[1,1024]{1,0:T(1,128)} %copy-done.64) | copy-start | bytes 12292
  114.5 15.7 %copy-start.67 = (f32[1,1024]{1,0:T(1,128)S(1)}, f32[1,1024]{1,0:T(1,128)}, u32[]{:S(2)}) copy-start(f32[1,1024]{1,0:T(1,128)} %copy-done.66) | copy-start | bytes 12292
  114.5 15.7 %copy-start.69 = (f32[1,1024]{1,0:T(1,128)S(1)}, f32[1,1024]{1,0:T(1,128)}, u32[]{:S(2)}) copy-start(f32[1,1024]{1,0:T(1,128)} %copy-done.68) | copy-start | bytes 12292
  115.2 9.4 %all-to-all-start.2 = ((bf16[4,128,128]{1,2,0:T(8,128)(2,1)}), bf16[4,128,128]{1,2,0:T(8,128)(2,1)S(1)}, u32[]{:S(2)}, u32[]{:S(2)}) async-start(bf16[4,128,128]{1,2,0:T(8,128)(2,1)} %copy.42), calls=%async_computation.2 | async-start | bytes 262144 | tf_op jit(solution)/shard_map/all_to_all | solution.py:207
  118.7 10.0 %collective-permute-start.3 = (bf16[1,1,8,16,1024]{4,3,2,1,0:T(8,128)(2,1)S(1)}, bf16[1,1,8,16,1024]{4,3,2,1,0:T(8,128)(2,1)S(1)}, u32[]{:S(2)}, u32[]{:S(2)}) collective-permute-start(bf16[1,1,8,16,1024]{4,3,2,1,0:T(8,128)(2,1)S(1)} %bitcast.245), channel_id=1, source_target_pairs={{4,0},{8,4},{12,8},{5,1},{9,5},{13,9},{6,2},{10,6},{14,10},{7,3},{... | collective-permute-start | bytes 786440 | tf_op jit(solution)/shard_map/ppermute | solution.py:19
  119.9 9.9 %collective-permute-start.2 = (bf16[1,1,8,16,1024]{4,3,2,1,0:T(8,128)(2,1)S(1)}, bf16[1,1,8,16,1024]{4,3,2,1,0:T(8,128)(2,1)S(1)}, u32[]{:S(2)}, u32[]{:S(2)}) collective-permute-start(bf16[1,1,8,16,1024]{4,3,2,1,0:T(8,128)(2,1)S(1)} %bitcast.246), channel_id=1, source_target_pairs={{0,4},{4,8},{8,12},{1,5},{5,9},{9,13},{2,6},{6,10},{10,14},{3,7},{... | collective-permute-start | bytes 786440 | tf_op jit(solution)/shard_map/ppermute | solution.py:18
  (28 other events, 182.2 us)
Sparse Core Ops, SparseCore 0:
  9.7 12.3 all-gather.6
  23.7 10.2 all-gather.10
  35.5 13.2 all-gather.8
  114.6 41.5 all-gather.12
